TPU v7x, 256 devices: a whole 4x4x8 slice. The times are simulated.
256 devices in a mesh: gx: 8 (over z), gy: 16 (over y, x), sa: 2 (over core).
Axes of the slice: x: 4, y: 4, z: 8, core: 2. Of those that a mesh axis runs over, the one named last changes fastest.
Arguments:
- field: float32 [33, 32, 672, 256], P(None, 'gx', 'gy', 'sa'), as said below
- start: float32 [33, 16], replicated, may hold values from -1 to 1
Outputs:
- basis: float32 [33, 16], replicated
- gram_two: float32 [672, 672], P('gy', ('gx', 'sa'))
Inputs may be any that keep to these rules, and one draw needn't show every extreme that they name: `field`: every entry is finite; species differ in scale.
All inputs are finite; a program needn't handle non-finite values.
Results may differ from a plain program's by a relative error of at most 0.0003.
Values sent between devices are 32-bit elements; how exact they have to be, the bound alone decides.
A program may use at most 128 MiB of HBM per device.

v0:
```python
import jax
import jax.numpy as jnp
from jax import lax
from jax.sharding import PartitionSpec as P

ITERS = 4
HIGH = lax.Precision.HIGHEST


def orth(block):
    inner = jnp.dot(block.T, block, precision=HIGH, preferred_element_type=jnp.float32)
    lower = jnp.linalg.cholesky(inner)
    return jax.scipy.linalg.solve_triangular(lower, block.T, lower=True).T


def leading(gram, start, rounds):
    basis = orth(orth(start))
    for step in range(rounds):
        basis = orth(orth(jnp.dot(gram, basis, precision=HIGH, preferred_element_type=jnp.float32)))
    return basis


def project(basis, data):
    return jnp.einsum("sr,sxyz->rxyz", basis, data, precision=HIGH)


def line_gram(left, right):
    return jnp.einsum("rxiz,rxjz->ij", left, right, precision=HIGH)


def on_device(field, start):
    species, cells_x, cells_y, cells_z = field.shape
    ranks = start.shape[1]
    total_x = cells_x * lax.axis_size("gx")
    total_y = cells_y * lax.axis_size("gy")
    total_z = cells_z * lax.axis_size("sa")
    flat = field.reshape(species, -1)
    partial_gram = jnp.dot(flat, flat.T, precision=HIGH, preferred_element_type=jnp.float32)
    species_gram = lax.psum(partial_gram, ("gx", "gy", "sa")) / (total_x * total_y * total_z)
    basis = leading(species_gram, start, ITERS)
    core = project(basis, field)
    part_block = line_gram(core, lax.all_gather(core, "gy", axis=2, tiled=True))
    block = lax.psum_scatter(part_block, ("gx", "sa"), scatter_dimension=1, tiled=True) / (
        ranks * total_x * total_z
    )
    return (basis, block)


def solution(mesh):
    in_specs = (P(None, "gx", "gy", "sa"), P())
    out_specs = (P(), P("gy", ("gx", "sa")))
    return jax.shard_map(
        on_device, mesh=mesh, in_specs=in_specs, out_specs=out_specs, check_vma=False
    )
```

profile of v0, /device:TPU:1, one launch (start us, length us, event | category | flops | bytes accessed | tf_op | source)
XLA Modules:
  0.0 422.5 jit_solution(17980562996375337005)
XLA Ops:
  7.2 0.6 copy-done
  8.1 1.5 cholesky.164
  9.6 0.6 compare_reduce_fusion.9
  10.2 0.6 fusion.27
  10.9 1.2 custom-call.14
  12.1 0.2 fusion.69
  12.5 1.5 cholesky.175
  14.0 0.6 compare_reduce_fusion.8
  14.7 0.6 fusion.28
  15.3 1.2 custom-call.15
  16.6 0.2 fusion.66
  16.8 6.2 %fusion.12 = f32[33,33]{1,0:T(8,128)S(1)} fusion(f32[33,4,42,128]{3,1,2,0:T(4,128)} %param.5), kind=kOutput, calls=%fused_computation.8 | convolution fusion | flops 281014272 | bytes 2842884 | tf_op jit(solution)/shard_map/dot_general | solution.py:38
  22.9 81.5 %psum.7 = f32[33,33]{1,0:T(8,128)S(1)} all-reduce(f32[33,33]{1,0:T(8,128)S(1)} %fusion.12), channel_id=1, replica_groups=mesh['gx'=8,'gy'=16,'sa'=2] {'gx','gy','sa'}, use_global_device_ids=true, to_apply=%region_0.0 | all-reduce | flops 1089 | bytes 8712 | tf_op jit(solution)/shard_map/psum | solution.py:39
  104.6 0.1 fusion.97
  104.8 1.5 cholesky.186
  106.3 0.6 compare_reduce_fusion.7
  107.0 0.6 fusion.29
  107.6 1.2 custom-call.16
  108.9 0.2 fusion.62
  109.3 1.5 cholesky.197
  110.8 0.6 compare_reduce_fusion.6
  111.4 0.6 fusion.30
  112.1 1.2 custom-call.17
  113.3 0.2 fusion.59
  113.5 0.2 fusion.19
  113.9 1.5 cholesky.208
  115.4 0.6 compare_reduce_fusion.5
  116.0 0.6 fusion.31
  116.7 1.2 custom-call.18
  117.9 0.2 fusion.55
  118.4 1.5 cholesky.219
  119.9 0.6 compare_reduce_fusion.4
  120.5 0.6 fusion.32
  121.2 1.2 custom-call.19
  122.4 0.2 fusion.52
  122.6 0.2 fusion.17
  123.0 1.5 cholesky.230
  124.5 0.6 compare_reduce_fusion.3
  125.1 0.6 fusion.33
  125.8 1.2 custom-call.20
  127.0 0.2 fusion.48
  127.4 1.5 cholesky.241
  128.9 0.6 compare_reduce_fusion.2
  129.6 0.6 fusion.34
  130.2 1.2 custom-call.21
  131.5 0.2 fusion.45
  131.7 0.2 fusion.15
  132.0 1.5 cholesky.252
  133.5 0.6 compare_reduce_fusion.1
  134.2 0.6 fusion.35
  134.9 1.2 custom-call.22
  136.1 0.2 fusion.41
  136.5 1.5 cholesky.263
  138.0 0.6 compare_reduce_fusion
  138.7 0.6 fusion.36
  139.3 1.2 custom-call.23
  140.5 0.2 fusion.38
  140.8 3.4 fusion.2
  144.2 0.2 all-reduce.3.cloned.1.call-start
  144.4 138.0 %all-gather.2.cloned.1.call-done = f32[16,4,672,128]{3,0,2,1:T(8,128)} async-done(((f32[16,4,42,128]{3,0,2,1:T(8,128)}), f32[16,4,672,128]{3,0,2,1:T(8,128)}) %all-gather.2.cloned.1.call-update) | async-done | bytes 22020112 | tf_op jit(solution)/shard_map/all_gather | solution.py:42
  282.4 29.2 %fusion.7 = f32[42,672]{1,0:T(8,128)} fusion(f32[16,4,672,128]{3,0,2,1:T(8,128)} %all-gather.2.cloned.1.call-done, f32[16,4,42,128]{3,0,2,1:T(8,128)} %fusion.2), kind=kOutput, calls=%fused_computation.7 | convolution fusion | flops 2774532096 | bytes 23509248 | tf_op jit(solution)/shard_map/rxiz,rxjz->ij/dot_general | solution.py:28
  311.6 0.6 dynamic-slice
  312.9 101.3 %all-reduce.3.cloned.1.call-done = f32[42,672]{1,0:T(8,128)} async-done(((f32[42,672]{1,0:T(8,128)}), f32[42,672]{1,0:T(8,128)}) %all-reduce.3.cloned.1.call-update) | async-done | bytes 112912
  414.2 1.5 dynamic-slice_multiply_fusion
  (50 shorter events, 2.6 us)
Async XLA Ops:
  7.2 0.7 copy-start
  7.2 133.6 %copy-start.1 = (f32[33,4,42,128]{3,1,2,0:T(4,128)S(1)}, f32[33,4,42,128]{3,1,2,0:T(4,128)}, u32[]{:S(2)}) copy-start(f32[33,4,42,128]{3,1,2,0:T(4,128)} %param.5) | copy-start | bytes 8515588
  7.2 275.2 %all-gather.2.cloned.1.call-start = ((), (), s32[]{:S(2)}) async-start(), calls=%async_computation | async-start | bytes 23396352 | tf_op jit(solution)/shard_map/all_gather | solution.py:42
  140.7 3.4 copy-start.2
  144.2 167.4 %copy-start.3 = (u32[256]{0:T(256)S(1)}, u32[256]{0:T(256)}, u32[]{:S(2)}) copy-start(u32[256]{0:T(256)} %constant.40) | copy-start | bytes 3076
  144.2 270.0 %all-reduce.3.cloned.1.call-start = ((), (), s32[]{:S(2)}) async-start(), calls=%async_computation.1 | async-start | bytes 294912
Sparse Core Ops, SparseCore 0:
  144.3 138.0 all-gather.1
  311.7 102.3 all-reduce.2
where the time goes:
time: 423 us; the launch traced here: 422 us
  waiting for transfers between devices  239 us (57%)
  blocking collectives  81.5 us (19%)
  matrix products  42.7 us (10%)
  other arithmetic  41.8 us (10%)
  between operations  14.9 us (4%)
    all_gather x1, waiting for transfers between devices, on_device(): part_block = line_gram(core, lax.all_gather(core, 'gy', axis=2, tiled=True))  138 us
    unnamed x3, waiting for transfers between devices  101 us
    psum x1, blocking collectives, on_device(): lax.psum(partial_gram, ('gx', 'gy', 'sa')) / (total_x * total_y * total_z)  81.5 us
    dot_general x1, matrix products, line_gram(): return jnp.einsum('rxiz,rxjz->ij', left, right, precision=HIGH)  29.2 us
    another operation x30, other arithmetic, orth(): lower = jnp.linalg.cholesky(inner)  21.5 us
    another operation x20, other arithmetic, orth(): return jax.scipy.linalg.solve_triangular(lower, block.T, lower=True).T  18.8 us
  transfers between devices with their start and end apart: 2, of which 2 were waited for; matrix products, arithmetic and copies ran while one was open for 0% of the time, Pallas kernels for 0%

commit v1 on v0

--- a/solution.py
+++ b/solution.py
@@ -1,3 +1,4 @@
+import functools
 import jax
 import jax.numpy as jnp
 from jax import lax
@@ -5,6 +6,15 @@
 
 ITERS = 4
 HIGH = lax.Precision.HIGHEST
+
+
+def _link_scenes(body, axis_id):
+    t1 = jnp.stack([body] * lax.axis_size(axis_id), axis=0)
+    y_new = lax.all_to_all(t1, axis_id, 0, 0)
+    return jnp.concatenate(y_new, axis=2)
+
+
+prepare_bench = functools.partial(_link_scenes, axis_id="gy")
 
 
 def orth(block):
@@ -39,7 +49,7 @@
     species_gram = lax.psum(partial_gram, ("gx", "gy", "sa")) / (total_x * total_y * total_z)
     basis = leading(species_gram, start, ITERS)
     core = project(basis, field)
-    part_block = line_gram(core, lax.all_gather(core, "gy", axis=2, tiled=True))
+    part_block = line_gram(core, prepare_bench(core))
     block = lax.psum_scatter(part_block, ("gx", "sa"), scatter_dimension=1, tiled=True) / (
         ranks * total_x * total_z
     )

time: 423 us -> 541 us (1.28)
  blocking collectives: 81.5 us -> 327 us
  waiting for transfers between devices: 239 us -> 98 us
  local copies, waits for them, and re-layouts: 1.98 us -> 19.6 us
    all_to_all x0 -> x1, blocking collectives: none -> 245 us  [_link_scenes(): y_new = lax.all_to_all(t1, axis_id, 0, 0)]
    all_gather x1 -> x0, waiting for transfers between devices: 138 us -> none  [on_device(): part_block = line_gram(core, lax.all_gather(core, 'gy', axis=2, tiled=True))]
    another operation x0 -> x1, local copies, waits for them, and re-layouts: none -> 9.98 us  [_link_scenes(): t1 = jnp.stack([body] * lax.axis_size(axis_id), axis=0)]
    all_to_all x0 -> x1, local copies, waits for them, and re-layouts: none -> 7.62 us  [_link_scenes(): y_new = lax.all_to_all(t1, axis_id, 0, 0)]
    unnamed x3 -> x2, waiting for transfers between devices: 101 us -> 98 us
  transfers between devices with their start and end apart: 2 -> 1, of which waited for: 2 -> 1; matrix products, arithmetic and copies ran while one was open for 0% -> 0% of each run, Pallas kernels for 0% -> 0%
where the time goes in v1:
time: 541 us
  blocking collectives  327 us (60%)
  waiting for transfers between devices  98 us (18%)
  other arithmetic  41.8 us (8%)
  matrix products  39.9 us (7%)
  local copies, waits for them, and re-layouts  19.6 us (4%)
  between operations  14.9 us (3%)
    all_to_all x1, blocking collectives, _link_scenes(): y_new = lax.all_to_all(t1, axis_id, 0, 0)  245 us
    unnamed x2, waiting for transfers between devices  98 us
    psum x1, blocking collectives, on_device(): lax.psum(partial_gram, ('gx', 'gy', 'sa')) / (total_x * total_y * total_z)  81.7 us
    dot_general x1, matrix products, line_gram(): return jnp.einsum('rxiz,rxjz->ij', left, right, precision=HIGH)  27.4 us
    another operation x30, other arithmetic, orth(): lower = jnp.linalg.cholesky(inner)  21.5 us
    another operation x20, other arithmetic, orth(): return jax.scipy.linalg.solve_triangular(lower, block.T, lower=True).T  18.8 us
  transfers between devices with their start and end apart: 1, of which 1 were waited for; matrix products, arithmetic and copies ran while one was open for 0% of the time, Pallas kernels for 0%

profile of v1, /device:TPU:1, one launch (start us, length us, event | category | flops | bytes accessed | tf_op | source)
XLA Modules:
  0.0 540.7 jit_solution(8105629635832154136)
XLA Ops:
  7.2 0.6 copy-done
  8.1 1.5 cholesky.164
  9.6 0.6 compare_reduce_fusion.9
  10.2 0.6 fusion.27
  10.9 1.2 custom-call.14
  12.1 0.2 fusion.69
  12.5 1.5 cholesky.175
  14.0 0.6 compare_reduce_fusion.8
  14.7 0.6 fusion.28
  15.3 1.2 custom-call.15
  16.6 0.2 fusion.66
  16.8 6.2 %fusion.12 = f32[33,33]{1,0:T(8,128)S(1)} fusion(f32[33,4,42,128]{3,1,2,0:T(4,128)} %param.5), kind=kOutput, calls=%fused_computation.8 | convolution fusion | flops 281014272 | bytes 2842884 | tf_op jit(solution)/shard_map/dot_general | solution.py:48
  22.9 81.7 %psum.7 = f32[33,33]{1,0:T(8,128)S(1)} all-reduce(f32[33,33]{1,0:T(8,128)S(1)} %fusion.12), channel_id=1, replica_groups=mesh['gx'=8,'gy'=16,'sa'=2] {'gx','gy','sa'}, use_global_device_ids=true, to_apply=%region_0.0 | all-reduce | flops 1089 | bytes 8712 | tf_op jit(solution)/shard_map/psum | solution.py:49
  105.0 1.5 cholesky.186
  106.5 0.6 compare_reduce_fusion.7
  107.2 0.6 fusion.29
  107.8 1.2 custom-call.16
  109.0 0.2 fusion.62
  109.5 1.5 cholesky.197
  111.0 0.6 compare_reduce_fusion.6
  111.6 0.6 fusion.30
  112.3 1.2 custom-call.17
  113.5 0.2 fusion.59
  113.7 0.2 fusion.19
  114.1 1.5 cholesky.208
  115.6 0.6 compare_reduce_fusion.5
  116.2 0.6 fusion.31
  116.9 1.2 custom-call.18
  118.1 0.2 fusion.55
  118.5 1.5 cholesky.219
  120.0 0.6 compare_reduce_fusion.4
  120.7 0.6 fusion.32
  121.4 1.2 custom-call.19
  122.6 0.2 fusion.52
  122.8 0.2 fusion.17
  123.2 1.5 cholesky.230
  124.7 0.6 compare_reduce_fusion.3
  125.3 0.6 fusion.33
  126.0 1.2 custom-call.20
  127.2 0.2 fusion.48
  127.6 1.5 cholesky.241
  129.1 0.6 compare_reduce_fusion.2
  129.8 0.6 fusion.34
  130.4 1.2 custom-call.21
  131.7 0.2 fusion.45
  131.9 0.2 fusion.15
  132.2 1.5 cholesky.252
  133.7 0.6 compare_reduce_fusion.1
  134.4 0.6 fusion.35
  135.0 1.2 custom-call.22
  136.3 0.2 fusion.41
  136.7 1.5 cholesky.263
  138.2 0.6 compare_reduce_fusion
  138.8 0.6 fusion.36
  139.5 1.2 custom-call.23
  140.7 0.2 fusion.38
  141.0 2.3 fusion.2
  143.2 10.0 %stack.2 = f32[16,16,4,42,128]{4,1,3,2,0:T(8,128)} broadcast(f32[16,4,42,128]{3,0,2,1:T(8,128)S(1)} %fusion.2), dimensions={1,2,3,4} | broadcast | bytes 23396352 | tf_op jit(solution)/shard_map/stack | solution.py:12
  153.2 244.8 %all_to_all.5 = f32[16,16,4,42,128]{4,1,3,2,0:T(8,128)S(1)} all-to-all(f32[16,16,4,42,128]{4,1,3,2,0:T(8,128)} %stack.2), channel_id=1, replica_groups=mesh['gx'=8,'gy'=16,'sa'=2] {'gy'}, dimensions={0} | all-to-all | bytes 44040192 | tf_op jit(solution)/shard_map/all_to_all | solution.py:13
  398.0 7.6 %copy.47 = f32[16,16,4,42,128]{4,1,3,0,2:T(8,128)} copy(f32[16,16,4,42,128]{4,1,3,2,0:T(8,128)S(1)} %all_to_all.5) | data formatting | bytes 44040192 | tf_op jit(solution)/shard_map/all_to_all | solution.py:13
  405.7 27.4 %fusion.7 = f32[42,672]{1,0:T(8,128)} fusion(f32[16,4,672,128]{3,0,2,1:T(8,128)} %bitcast.154, f32[16,4,42,128]{3,0,2,1:T(8,128)S(1)} %fusion.2), kind=kOutput, calls=%fused_computation.7 | convolution fusion | flops 2774532096 | bytes 23509248 | tf_op jit(solution)/shard_map/rxiz,rxjz->ij/dot_general | solution.py:38
  433.1 0.6 dynamic-slice
  434.4 98.0 %all-reduce.3.cloned.1.call-done = f32[42,672]{1,0:T(8,128)} async-done(((f32[42,672]{1,0:T(8,128)}), f32[42,672]{1,0:T(8,128)}) %all-reduce.3.cloned.1.call-update) | async-done | bytes 112912
  532.3 1.5 dynamic-slice_multiply_fusion
  (52 shorter events, 2.7 us)
Async XLA Ops:
  7.2 0.7 copy-start
  7.2 133.8 %copy-start.2 = (f32[33,4,42,128]{3,1,2,0:T(4,128)S(1)}, f32[33,4,42,128]{3,1,2,0:T(4,128)}, u32[]{:S(2)}) copy-start(f32[33,4,42,128]{3,1,2,0:T(4,128)} %param.5) | copy-start | bytes 8515588
  7.2 525.1 %all-reduce.3.cloned.1.call-start = ((), (), s32[]{:S(2)}) async-start(), calls=%async_computation.1 | async-start | bytes 294912
  140.9 12.3 %copy-start.3 = (f32[16,33]{1,0:T(8,128)}, f32[16,33]{1,0:T(8,128)S(1)}, u32[]{:S(2)}) copy-start(f32[16,33]{1,0:T(8,128)S(1)} %fusion.38) | copy-start | bytes 6340
  405.7 27.5 %copy-start.4 = (u32[256]{0:T(256)S(1)}, u32[256]{0:T(256)}, u32[]{:S(2)}) copy-start(u32[256]{0:T(256)} %constant.40) | copy-start | bytes 3076
  405.7 128.2 %copy-start.1 = (f32[33,16]{0,1:T(8,128)S(1)}, f32[33,16]{0,1:T(8,128)}, u32[]{:S(2)}) copy-start(f32[33,16]{0,1:T(8,128)} %param.6) | copy-start | bytes 6340
Sparse Core Ops, SparseCore 0:
  433.2 99.0 all-reduce.2
